TPU v7x, 128 devices: a whole 4x4x4 slice. The times are simulated.
128 devices in a mesh: leaf: 16 (over x, y), side: 8 (over z, core).
Axes of the slice: x: 4, y: 4, z: 4, core: 2. Of those that a mesh axis runs over, the one named last changes fastest.
Arguments:
- block: float32 [131072, 512], P(('leaf', 'side')), may hold values from -24 to 24
- basis: float32 [131072, 1024], P(('leaf', 'side')), may hold values from -1 to 1
Outputs:
- ortho: float32 [131072, 512], P(('leaf', 'side'))
- factor: float32 [512, 512], replicated
- coeffs: float32 [1024, 512], replicated
All inputs are finite; a program needn't handle non-finite values.
Results may differ from a plain program's by a relative error of at most 0.0001.
Values sent between devices are 32-bit elements; how exact they have to be, the bound alone decides.
A program may use at most 64 MiB of HBM per device.

v0:
```python
import jax
import jax.numpy as jnp
from jax import lax
from jax.sharding import PartitionSpec as P


def inner(left, right):
    return lax.dot_general(
        left,
        right,
        (((0,), (0,)), ((), ())),
        precision=lax.Precision.HIGHEST,
        preferred_element_type=jnp.float32,
    )


def product(left, right):
    return jnp.dot(left, right, precision=lax.Precision.HIGHEST, preferred_element_type=jnp.float32)


def small_upper(matrix):
    width = matrix.shape[0]
    positions = jnp.arange(width, dtype=jnp.int32)

    def one_step(column, carry):
        rest, result = carry
        column = jnp.asarray(column).astype(jnp.int32)
        row = lax.dynamic_slice_in_dim(rest, column, 1, 0)[0]
        pivot = jnp.sqrt(jnp.sum(jnp.where(positions == column, row, jnp.float32(0.0))))
        new_row = jnp.where(positions >= column, row / pivot, jnp.float32(0.0))
        result = lax.dynamic_update_slice_in_dim(result, new_row[None, :], column, 0)
        rest = rest - new_row[:, None] * new_row[None, :]
        return (rest, result)

    start = (matrix, jnp.zeros_like(matrix))
    return lax.fori_loop(0, width, one_step, start)[1]


def small_inverse(upper_block):
    width = upper_block.shape[0]
    positions = jnp.arange(width, dtype=jnp.int32)

    def one_step(count, result):
        index = (width - 1 - jnp.asarray(count)).astype(jnp.int32)
        row = lax.dynamic_slice_in_dim(upper_block, index, 1, 0)[0]
        pivot = jnp.sum(jnp.where(positions == index, row, jnp.float32(0.0)))
        beyond = jnp.where(positions > index, row, jnp.float32(0.0))
        unit = jnp.where(positions == index, jnp.float32(1.0), jnp.float32(0.0))
        new_row = (unit - product(beyond[None, :], result)[0]) / pivot
        return lax.dynamic_update_slice_in_dim(result, new_row[None, :], index, 0)

    return lax.fori_loop(0, width, one_step, jnp.zeros_like(upper_block))


def factor_and_inverse(gram):
    width = gram.shape[0]
    piece = min(128, width)
    count = width // piece
    rest = gram
    strips = []
    diag_inverses = []
    for index in range(count):
        diag = small_upper(rest[:piece, :piece])
        diag_inv = small_inverse(diag)
        right = product(diag_inv.T, rest[:piece, piece:])
        left_zeros = jnp.zeros((piece, index * piece), gram.dtype)
        strips.append(jnp.concatenate([left_zeros, diag, right], axis=1))
        diag_inverses.append(diag_inv)
        rest = rest[piece:, piece:] - inner(right, right)
    factor = jnp.concatenate(strips, axis=0)
    lower_part = None
    for index in reversed(range(count)):
        diag_inv = diag_inverses[index]
        if lower_part is None:
            lower_part = diag_inv
        else:
            coupling = factor[index * piece : (index + 1) * piece, (index + 1) * piece :]
            far = -product(diag_inv, product(coupling, lower_part))
            top = jnp.concatenate([diag_inv, far], axis=1)
            below = jnp.concatenate(
                [jnp.zeros((lower_part.shape[0], piece), gram.dtype), lower_part], axis=1
            )
            lower_part = jnp.concatenate([top, below], axis=0)
    return (factor, lower_part)


def shards(block, basis):
    rows_total = block.shape[0] * lax.axis_size("leaf") * lax.axis_size("side")
    coeffs = lax.psum(inner(basis, block), ("leaf", "side"))
    projected = block - product(basis, coeffs)
    local_gram = inner(projected, projected) / rows_total
    factor, inverse = factor_and_inverse(lax.psum(local_gram, ("leaf", "side")))
    ortho = product(projected, inverse)
    return (ortho, factor, coeffs)


def solution(mesh):
    return jax.shard_map(
        shards,
        mesh=mesh,
        in_specs=(P(("leaf", "side"), None), P(("leaf", "side"), None)),
        out_specs=(P(("leaf", "side"), None), P(), P()),
        check_vma=False,
    )
```

profile of v0, /device:TPU:1, one launch (start us, length us, event | category | flops | bytes accessed | tf_op | source)
XLA Modules:
  0.0 1886.3 jit_solution(14410040137876746820)
XLA Ops:
  7.2 10.2 fusion.74
  17.7 1.3 copy-done
  19.0 1.8 copy.5
  20.8 150.3 %all-reduce.7.cloned.1.call-done = f32[1024,512]{1,0:T(8,128)} async-done(((f32[1024,512]{1,0:T(8,128)}), f32[1024,512]{1,0:T(8,128)}) %all-reduce.7.cloned.1.call-update) | async-done | bytes 2097168 | tf_op jit(solution)/shard_map/psum | solution.py:89
  171.2 16.2 bitcast_subtract_fusion
  187.3 4.5 convolution_multiply_fusion
  191.8 145.8 %all-reduce.9.cloned.1.call-done = f32[512,512]{1,0:T(8,128)} async-done(((f32[512,512]{1,0:T(8,128)}), f32[512,512]{1,0:T(8,128)}) %all-reduce.9.cloned.1.call-update) | async-done | bytes 1048592 | tf_op jit(solution)/shard_map/psum | solution.py:92
  337.6 0.8 slice.36
  338.5 192.5 %while.136 = (s32[]{:T(128)}, f32[128,128]{1,0:T(8,128)S(1)}, f32[128,128]{1,0:T(8,128)S(1)}, s32[]{:T(128)}, s32[]{:T(128)}) while((s32[]{:T(128)}, f32[128,128]{1,0:T(8,128)S(1)}, f32[128,128]{1,0:T(8,128)S(1)}, s32[]{:T(128)}, s32[]{:T(128)}) %tuple.273), condition=%wide.region_4.5_spmd.clone.clone, body=%wide.region_2.4_spmd.clone.clone.sunk | while | flops 34305 | bytes 142421 | solution.py:36
  531.0 187.3 %while.137 = (s32[]{:T(128)}, f32[128,128]{1,0:T(8,128)S(1)}, f32[128,128]{1,0:T(8,128)S(1)}, s32[]{:T(128)}, s32[]{:T(128)}, /*index=5*/s32[]{:T(128)}, s32[]{:T(128)}) while((s32[]{:T(128)}, f32[128,128]{1,0:T(8,128)S(1)}, f32[128,128]{1,0:T(8,128)S(1)}, s32[]{:T(128)}, s32[]{:T(128)}, /*index=5*/s32[]{:T(128)}, ...), condition=%wide.region_7.8_spmd.clone.clone, body=%wide.region_5.7_spmd.clone.clone.sunk | while | flops 197765 | bytes 69783 | solution.py:52
  531.6 0.8 fusion.139
  557.9 0.8 fusion.139
  559.4 0.8 fusion.139
  585.7 0.8 fusion.139
  587.1 0.8 fusion.139
  613.4 0.8 fusion.139
  614.9 0.8 fusion.139
  641.2 0.8 fusion.139
  642.7 0.8 fusion.139
  669.0 0.8 fusion.139
  670.4 0.8 fusion.139
  696.8 0.8 fusion.139
  698.2 0.8 fusion.139
  718.9 1.3 fusion.63
  720.2 1.7 convolution_subtract_fusion
  722.0 192.5 %while.138 = (s32[]{:T(128)}, f32[128,128]{1,0:T(8,128)S(1)}, f32[128,128]{1,0:T(8,128)S(1)}, s32[]{:T(128)}, s32[]{:T(128)}) while((s32[]{:T(128)}, f32[128,128]{1,0:T(8,128)S(1)}, f32[128,128]{1,0:T(8,128)S(1)}, s32[]{:T(128)}, s32[]{:T(128)}) %tuple.279), condition=%wide.region_10.11_spmd.clone.clone, body=%wide.region_8.10_spmd.clone.clone.sunk | while | flops 34305 | bytes 142421 | solution.py:36
  914.5 187.1 %while.139 = (s32[]{:T(128)}, f32[128,128]{1,0:T(8,128)S(1)}, f32[128,128]{1,0:T(8,128)S(1)}, s32[]{:T(128)}, s32[]{:T(128)}, /*index=5*/s32[]{:T(128)}, s32[]{:T(128)}) while((s32[]{:T(128)}, f32[128,128]{1,0:T(8,128)S(1)}, f32[128,128]{1,0:T(8,128)S(1)}, s32[]{:T(128)}, s32[]{:T(128)}, /*index=5*/s32[]{:T(128)}, ...), condition=%wide.region_13.14_spmd.clone.clone, body=%wide.region_11.13_spmd.clone.clone.sunk | while | flops 197765 | bytes 69783 | solution.py:52
  918.0 0.8 fusion.145
  919.5 0.8 fusion.145
  945.8 0.8 fusion.145
  947.2 0.8 fusion.145
  973.5 0.8 fusion.145
  975.0 0.8 fusion.145
  1001.3 0.8 fusion.145
  1002.8 0.8 fusion.145
  1029.1 0.8 fusion.145
  1030.5 0.8 fusion.145
  1056.9 0.8 fusion.145
  1058.3 0.8 fusion.145
  1084.6 0.8 fusion.145
  1086.1 0.8 fusion.145
  1102.9 192.5 %while.140 = (s32[]{:T(128)}, f32[128,128]{1,0:T(8,128)S(1)}, f32[128,128]{1,0:T(8,128)S(1)}, s32[]{:T(128)}, s32[]{:T(128)}) while((s32[]{:T(128)}, f32[128,128]{1,0:T(8,128)S(1)}, f32[128,128]{1,0:T(8,128)S(1)}, s32[]{:T(128)}, s32[]{:T(128)}) %tuple.285), condition=%wide.region_16.17_spmd.clone.clone, body=%wide.region_14.16_spmd.clone.clone.sunk | while | flops 34305 | bytes 142421 | solution.py:36
  1295.4 187.1 %while.141 = (s32[]{:T(128)}, f32[128,128]{1,0:T(8,128)S(1)}, f32[128,128]{1,0:T(8,128)S(1)}, s32[]{:T(128)}, s32[]{:T(128)}, /*index=5*/s32[]{:T(128)}, s32[]{:T(128)}) while((s32[]{:T(128)}, f32[128,128]{1,0:T(8,128)S(1)}, f32[128,128]{1,0:T(8,128)S(1)}, s32[]{:T(128)}, s32[]{:T(128)}, /*index=5*/s32[]{:T(128)}, ...), condition=%wide.region_19.20_spmd.clone.clone, body=%wide.region_17.19_spmd.clone.clone.sunk | while | flops 197765 | bytes 69783 | solution.py:52
  1304.8 0.8 fusion.151
  1306.3 0.8 fusion.151
  1332.6 0.8 fusion.151
  1334.0 0.8 fusion.151
  1360.4 0.8 fusion.151
  1361.8 0.8 fusion.151
  1388.1 0.8 fusion.151
  1389.6 0.8 fusion.151
  1415.9 0.8 fusion.151
  1417.4 0.8 fusion.151
  1443.7 0.8 fusion.151
  1445.1 0.8 fusion.151
  1471.4 0.8 fusion.151
  1483.7 192.5 %while.142 = (s32[]{:T(128)}, f32[128,128]{1,0:T(8,128)S(1)}, f32[128,128]{1,0:T(8,128)S(1)}, s32[]{:T(128)}, s32[]{:T(128)}) while((s32[]{:T(128)}, f32[128,128]{1,0:T(8,128)S(1)}, f32[128,128]{1,0:T(8,128)S(1)}, s32[]{:T(128)}, s32[]{:T(128)}) %tuple.291), condition=%wide.region_22.23_spmd.clone.clone, body=%wide.region_20.22_spmd.clone.clone.sunk | while | flops 34305 | bytes 142421 | solution.py:36
  1676.3 187.1 %while.143 = (s32[]{:T(128)}, f32[128,128]{1,0:T(8,128)S(1)}, f32[128,128]{1,0:T(8,128)S(1)}, s32[]{:T(128)}, s32[]{:T(128)}, /*index=5*/s32[]{:T(128)}, s32[]{:T(128)}) while((s32[]{:T(128)}, f32[128,128]{1,0:T(8,128)S(1)}, f32[128,128]{1,0:T(8,128)S(1)}, s32[]{:T(128)}, s32[]{:T(128)}, /*index=5*/s32[]{:T(128)}, ...), condition=%wide.region_25.26_spmd.clone.clone, body=%wide.region_23.25_spmd.clone.clone.sunk | while | flops 197765 | bytes 69783 | solution.py:52
  1865.1 1.4 fusion.73
  1866.7 1.4 convolution_negate_fusion
  1868.2 8.0 fusion.56
  1876.2 1.1 select_maximum_fusion
  1877.3 0.8 copy-done.1
  1878.1 1.3 copy.83
  (4617 shorter events, 1100.8 us)
Async XLA Ops:
  7.2 164.0 %all-reduce.7.cloned.1.call-start = ((), (), s32[]{:S(2)}) async-start(), calls=%async_computation | async-start | bytes 4194304 | tf_op jit(solution)/shard_map/psum | solution.py:89
  17.4 1.6 copy-start
  17.4 320.2 %all-reduce.9.cloned.1.call-start = ((), (), s32[]{:S(2)}) async-start(), calls=%async_computation.1 | async-start | bytes 2097152 | tf_op jit(solution)/shard_map/psum | solution.py:92
  718.3 0.6 copy-start.2
  1101.5 0.6 copy-start.4
  1482.5 0.6 copy-start.6
  1863.3 1.3 copy-start.8
  1868.1 8.1 copy-start.3
  1868.1 8.1 copy-start.5
  1868.2 8.1 copy-start.7
  1868.2 8.1 copy-start.9
  1876.2 2.0 copy-start.1
Sparse Core Ops, SparseCore 0:
  17.6 153.5 all-reduce.6
  192.0 145.6 all-reduce.8
where the time goes:
time: 1900 us; the launch traced here: 1890 us
  other arithmetic  685 us (36%)
  matrix products  455 us (24%)
  loops' own time  391 us (21%)
  waiting for transfers between devices  296 us (16%)
  local copies, waits for them, and re-layouts  43.5 us (2%)
    dot_general x523, matrix products, product(): jnp.dot(left, right, precision=lax.Precision.HIGHEST, preferred_element_t...  438 us
    another operation x4, loops' own time, small_upper(): return lax.fori_loop(0, width, one_step, start)[1]  377 us
    reduce_sum x512, other arithmetic, one_step(): pivot = jnp.sum(jnp.where(positions == index, row, jnp.float32(0.0)))  311 us
    reduce_sum x512, other arithmetic, one_step(): jnp.sum(jnp.where(positions == column, row, jnp.float32(0.0)))  310 us
    psum x1, waiting for transfers between devices, shards(): coeffs = lax.psum(inner(basis, block), ('leaf', 'side'))  150 us
    psum x1, waiting for transfers between devices, shards(): factor, inverse = factor_and_inverse(lax.psum(local_gram, ('leaf', 'side')))  146 us
    sub x512, other arithmetic, one_step(): rest = rest - new_row[:, None] * new_row[None, :]  42.1 us

commit v1 on v0

--- a/solution.py
+++ b/solution.py
@@ -89,7 +89,7 @@
     coeffs = lax.psum(inner(basis, block), ("leaf", "side"))
     projected = block - product(basis, coeffs)
     local_gram = inner(projected, projected) / rows_total
-    factor, inverse = factor_and_inverse(lax.psum(local_gram, ("leaf", "side")))
+    factor, inverse = factor_and_inverse(lax.psum(lax.psum(local_gram, "leaf"), "side"))
     ortho = product(projected, inverse)
     return (ortho, factor, coeffs)
 

time: 1900 us -> 1840 us (0.968)
  matrix products: 455 us -> 426 us
  loops' own time: 391 us -> 362 us
    dot_general x523, matrix products: 438 us -> 409 us  [product(): jnp.dot(left, right, precision=lax.Precision.HIGHEST, preferred_element_t...]
    another operation x4, loops' own time: 377 us -> 348 us  [small_upper(): return lax.fori_loop(0, width, one_step, start)[1]]
    psum x1 -> x2, waiting for transfers between devices: 146 us -> 147 us  [the longest x1 83.5 us: shards(): lax.psum(local_gram, 'leaf')]
where the time goes in v1:
time: 1840 us; the launch traced here: 1830 us
  other arithmetic  684 us (37%)
  matrix products  426 us (23%)
  loops' own time  362 us (20%)
  waiting for transfers between devices  298 us (16%)
  local copies, waits for them, and re-layouts  43.5 us (2%)
    dot_general x523, matrix products, product(): jnp.dot(left, right, precision=lax.Precision.HIGHEST, preferred_element_t...  409 us
    another operation x4, loops' own time, small_upper(): return lax.fori_loop(0, width, one_step, start)[1]  348 us
    reduce_sum x512, other arithmetic, one_step(): pivot = jnp.sum(jnp.where(positions == index, row, jnp.float32(0.0)))  310 us
    reduce_sum x512, other arithmetic, one_step(): jnp.sum(jnp.where(positions == column, row, jnp.float32(0.0)))  309 us
    psum x1, waiting for transfers between devices, shards(): coeffs = lax.psum(inner(basis, block), ('leaf', 'side'))  150 us
    psum x1, waiting for transfers between devices, shards(): lax.psum(local_gram, 'leaf')  83.5 us
    psum x1, waiting for transfers between devices, shards(): lax.psum(lax.psum(local_gram, 'leaf'), 'side')  63.7 us
    sub x512, other arithmetic, one_step(): rest = rest - new_row[:, None] * new_row[None, :]  42.1 us

profile of v1, /device:TPU:1, one launch (start us, length us, event | category | flops | bytes accessed | tf_op | source)
XLA Modules:
  0.0 1827.6 jit_solution(16015379351258437922)
XLA Ops:
  7.2 10.2 fusion.74
  17.7 1.3 copy-done
  19.0 1.8 copy.5
  20.8 150.3 %all-reduce.8.cloned.1.call-done = f32[1024,512]{1,0:T(8,128)} async-done(((f32[1024,512]{1,0:T(8,128)}), f32[1024,512]{1,0:T(8,128)}) %all-reduce.8.cloned.1.call-update) | async-done | bytes 2097168 | tf_op jit(solution)/shard_map/psum | solution.py:89
  171.2 16.2 bitcast_subtract_fusion
  187.3 4.5 convolution_multiply_fusion
  192.1 83.5 %all-reduce.10.cloned.1.call-done = f32[512,512]{1,0:T(8,128)} async-done(((f32[512,512]{1,0:T(8,128)}), f32[512,512]{1,0:T(8,128)}) %all-reduce.10.cloned.1.call-update) | async-done | bytes 1048592 | tf_op jit(solution)/shard_map/psum | solution.py:92
  275.7 63.7 %all-reduce.12.cloned.1.call-done = f32[512,512]{1,0:T(8,128)} async-done(((f32[512,512]{1,0:T(8,128)}), f32[512,512]{1,0:T(8,128)}) %all-reduce.12.cloned.1.call-update) | async-done | bytes 1048592 | tf_op jit(solution)/shard_map/psum | solution.py:92
  339.4 0.8 slice.36
  340.3 175.1 %while.136 = (s32[]{:T(128)}, f32[128,128]{1,0:T(8,128)S(1)}, f32[128,128]{1,0:T(8,128)S(1)}, s32[]{:T(128)}, s32[]{:T(128)}) while((s32[]{:T(128)}, f32[128,128]{1,0:T(8,128)S(1)}, f32[128,128]{1,0:T(8,128)S(1)}, s32[]{:T(128)}, s32[]{:T(128)}) %tuple.273), condition=%wide.region_5.6_spmd.clone.clone, body=%wide.region_3.5_spmd.clone.clone.sunk | while | flops 34305 | bytes 142421 | solution.py:36
  515.4 169.7 %while.137 = (s32[]{:T(128)}, f32[128,128]{1,0:T(8,128)S(1)}, f32[128,128]{1,0:T(8,128)S(1)}, s32[]{:T(128)}, s32[]{:T(128)}, /*index=5*/s32[]{:T(128)}, s32[]{:T(128)}) while((s32[]{:T(128)}, f32[128,128]{1,0:T(8,128)S(1)}, f32[128,128]{1,0:T(8,128)S(1)}, s32[]{:T(128)}, s32[]{:T(128)}, /*index=5*/s32[]{:T(128)}, ...), condition=%wide.region_8.9_spmd.clone.clone, body=%wide.region_6.8_spmd.clone.clone.sunk | while | flops 197765 | bytes 69783 | solution.py:52
  685.7 1.3 fusion.63
  687.0 1.7 convolution_subtract_fusion
  688.8 176.4 %while.138 = (s32[]{:T(128)}, f32[128,128]{1,0:T(8,128)S(1)}, f32[128,128]{1,0:T(8,128)S(1)}, s32[]{:T(128)}, s32[]{:T(128)}) while((s32[]{:T(128)}, f32[128,128]{1,0:T(8,128)S(1)}, f32[128,128]{1,0:T(8,128)S(1)}, s32[]{:T(128)}, s32[]{:T(128)}) %tuple.279), condition=%wide.region_11.12_spmd.clone.clone, body=%wide.region_9.11_spmd.clone.clone.sunk | while | flops 34305 | bytes 142421 | solution.py:36
  865.2 171.0 %while.139 = (s32[]{:T(128)}, f32[128,128]{1,0:T(8,128)S(1)}, f32[128,128]{1,0:T(8,128)S(1)}, s32[]{:T(128)}, s32[]{:T(128)}, /*index=5*/s32[]{:T(128)}, s32[]{:T(128)}) while((s32[]{:T(128)}, f32[128,128]{1,0:T(8,128)S(1)}, f32[128,128]{1,0:T(8,128)S(1)}, s32[]{:T(128)}, s32[]{:T(128)}, /*index=5*/s32[]{:T(128)}, ...), condition=%wide.region_14.15_spmd.clone.clone, body=%wide.region_12.14_spmd.clone.clone.sunk | while | flops 197765 | bytes 69783 | solution.py:52
  1037.5 196.0 %while.140 = (s32[]{:T(128)}, f32[128,128]{1,0:T(8,128)S(1)}, f32[128,128]{1,0:T(8,128)S(1)}, s32[]{:T(128)}, s32[]{:T(128)}) while((s32[]{:T(128)}, f32[128,128]{1,0:T(8,128)S(1)}, f32[128,128]{1,0:T(8,128)S(1)}, s32[]{:T(128)}, s32[]{:T(128)}) %tuple.285), condition=%wide.region_17.18_spmd.clone.clone, body=%wide.region_15.17_spmd.clone.clone.sunk | while | flops 34305 | bytes 142421 | solution.py:36
  1233.5 190.6 %while.141 = (s32[]{:T(128)}, f32[128,128]{1,0:T(8,128)S(1)}, f32[128,128]{1,0:T(8,128)S(1)}, s32[]{:T(128)}, s32[]{:T(128)}, /*index=5*/s32[]{:T(128)}, s32[]{:T(128)}) while((s32[]{:T(128)}, f32[128,128]{1,0:T(8,128)S(1)}, f32[128,128]{1,0:T(8,128)S(1)}, s32[]{:T(128)}, s32[]{:T(128)}, /*index=5*/s32[]{:T(128)}, ...), condition=%wide.region_20.21_spmd.clone.clone, body=%wide.region_18.20_spmd.clone.clone.sunk | while | flops 197765 | bytes 69783 | solution.py:52
  1425.3 192.5 %while.142 = (s32[]{:T(128)}, f32[128,128]{1,0:T(8,128)S(1)}, f32[128,128]{1,0:T(8,128)S(1)}, s32[]{:T(128)}, s32[]{:T(128)}) while((s32[]{:T(128)}, f32[128,128]{1,0:T(8,128)S(1)}, f32[128,128]{1,0:T(8,128)S(1)}, s32[]{:T(128)}, s32[]{:T(128)}) %tuple.291), condition=%wide.region_23.24_spmd.clone.clone, body=%wide.region_21.23_spmd.clone.clone.sunk | while | flops 34305 | bytes 142421 | solution.py:36
  1617.9 187.1 %while.143 = (s32[]{:T(128)}, f32[128,128]{1,0:T(8,128)S(1)}, f32[128,128]{1,0:T(8,128)S(1)}, s32[]{:T(128)}, s32[]{:T(128)}, /*index=5*/s32[]{:T(128)}, s32[]{:T(128)}) while((s32[]{:T(128)}, f32[128,128]{1,0:T(8,128)S(1)}, f32[128,128]{1,0:T(8,128)S(1)}, s32[]{:T(128)}, s32[]{:T(128)}, /*index=5*/s32[]{:T(128)}, ...), condition=%wide.region_26.27_spmd.clone.clone, body=%wide.region_24.26_spmd.clone.clone.sunk | while | flops 197765 | bytes 69783 | solution.py:52
  1618.5 0.8 fusion.157
  1619.9 0.8 fusion.157
  1621.4 0.8 fusion.157
  1622.9 0.8 fusion.157
  1624.3 0.8 fusion.157
  1625.8 0.8 fusion.157
  1627.3 0.8 fusion.157
  1628.7 0.8 fusion.157
  1630.2 0.8 fusion.157
  1631.6 0.8 fusion.157
  1633.1 0.8 fusion.157
  1634.6 0.8 fusion.157
  1636.0 0.8 fusion.157
  1637.5 0.8 fusion.157
  1638.9 0.8 fusion.157
  1640.4 0.8 fusion.157
  1641.9 0.8 fusion.157
  1643.3 0.8 fusion.157
  1644.8 0.8 fusion.157
  1646.3 0.8 fusion.157
  1647.7 0.8 fusion.157
  1649.2 0.8 fusion.157
  1650.6 0.8 fusion.157
  1652.1 0.8 fusion.157
  1653.6 0.8 fusion.157
  1655.0 0.8 fusion.157
  1656.5 0.8 fusion.157
  1657.9 0.8 fusion.157
  1659.4 0.8 fusion.157
  1684.3 0.8 fusion.157
  1685.7 0.8 fusion.157
  1712.0 0.8 fusion.157
  1713.5 0.8 fusion.157
  1739.8 0.8 fusion.157
  1741.3 0.8 fusion.157
  1767.6 0.8 fusion.157
  1769.0 0.8 fusion.157
  1795.3 0.8 fusion.157
  1796.8 0.8 fusion.157
  1806.7 1.4 fusion.73
  1808.3 1.4 convolution_negate_fusion
  1809.8 8.0 fusion.56
  1817.8 1.1 select_maximum_fusion
  1818.9 0.8 copy-done.1
  1819.7 1.3 copy.84
  (4620 shorter events, 1070.9 us)
Async XLA Ops:
  7.2 164.0 %all-reduce.8.cloned.1.call-start = ((), (), s32[]{:S(2)}) async-start(), calls=%async_computation | async-start | bytes 4194304 | tf_op jit(solution)/shard_map/psum | solution.py:89
  17.4 1.6 copy-start
  17.4 258.2 %all-reduce.10.cloned.1.call-start = ((), (), s32[]{:S(2)}) async-start(), calls=%async_computation.1 | async-start | bytes 2097152 | tf_op jit(solution)/shard_map/psum | solution.py:92
  191.8 147.6 %all-reduce.12.cloned.1.call-start = ((), (), s32[]{:S(2)}) async-start(), calls=%async_computation.2 | async-start | bytes 2097152 | tf_op jit(solution)/shard_map/psum | solution.py:92
  685.1 0.6 copy-start.2
  1036.1 0.6 copy-start.4
  1424.1 0.6 copy-start.6
  1804.9 1.3 copy-start.8
  1809.7 8.1 copy-start.3
  1809.7 8.1 copy-start.5
  1809.8 8.1 copy-start.7
  1809.8 8.1 copy-start.9
  1817.8 2.0 copy-start.1
Sparse Core Ops, SparseCore 0:
  17.6 153.5 all-reduce.7
  192.0 83.6 all-reduce.9
  278.0 61.3 all-reduce.11
